TPU v7x, 128 devices: a whole 4x4x4 slice. The times are simulated.
128 devices in a mesh: section: 4 (over x), dev: 32 (over y, z, core).
Axes of the slice: x: 4, y: 4, z: 4, core: 2. Of those that a mesh axis runs over, the one named last changes fastest.
Arguments:
- hidden: bfloat16 [1024, 2048], P('dev'), may hold values from -8 to 8
- lengths: int32 [1024], P('dev'), may hold values from 1 to 256, as said below
- attn_gain: float32 [2048], replicated, may hold values from 0.1 to 1.9
- w_query: bfloat16 [2048, 3072], P(None, 'section'), may hold values from -0.125 to 0.125
- w_latent: bfloat16 [2048, 512], replicated, may hold values from -0.125 to 0.125
- latent_gain: float32 [512], replicated, may hold values from 0.1 to 1.9
- w_rope_key: bfloat16 [64, 2048], replicated, may hold values from -0.125 to 0.125
- w_key_up: bfloat16 [16, 512, 128], P('section'), may hold values from -0.5 to 0.5
- w_value_up: bfloat16 [16, 512, 128], P('section'), may hold values from -0.25 to 0.25
- w_out: bfloat16 [2048, 2048], P('section'), may hold values from -0.125 to 0.125
- latent_cache: bfloat16 [1024, 256, 512], P('dev'), may hold values from -6 to 6
- rope_cache: bfloat16 [1024, 64, 256], P('dev'), may hold values from -1200 to 1200
- ffn_gain: float32 [2048], replicated, may hold values from 0.1 to 1.9
- expert_ids: int32 [1024, 6], P('dev'), may hold values from 0 to 63, all different within a row; in each aligned block of 8 rows (0 to 7, 8 to 15, ...) at most 2 rows name the same one
- route_weights: float32 [1024, 6], P('dev'), may hold values from 0.05 to 0.5
- w_gate_up: bfloat16 [64, 2, 1408, 2048], P('dev', None, 'section'), may hold values from -0.125 to 0.125
- w_down: bfloat16 [64, 1408, 2048], P('dev', 'section'), may hold values from -0.15625 to 0.15625
Outputs:
- layer_out: bfloat16 [1024, 2048], P('dev')
Inputs may be any that keep to these rules, and one draw needn't show every extreme that they name: `lengths`: every aligned block of 32 rows holds a row of length 256. `expert_ids`: each row names 6 different experts. In every aligned block of 8 rows no expert is named by more than 2 rows, and some block has an expert named by exactly 2.
All inputs are finite; a program needn't handle non-finite values.
Results may differ from a plain program's by a relative error of at most 0.011.
Values may be sent and summed in bfloat16 or wider, within the bound.
No kernel may reach another device: no remote copies, remote signals or barrier semaphores. Data moves between devices by JAX's collectives and lax.ppermute only.
A program may use at most 128 MiB of HBM per device.

v0:
```python
import jax
import jax.numpy as jnp
from jax import lax
from jax.sharding import PartitionSpec as P

EXPERTS = 64
MOST = 2
epsilon = 1e-06
far_below = -1e30


def rms_norm(values, norm_gain):
    mean_square = jnp.mean(values * values, axis=-1, keepdims=True)
    return values * lax.rsqrt(mean_square + epsilon) * norm_gain


def rotary(values, positions):
    half_width = values.shape[-1] // 2
    step_index = jnp.arange(half_width, dtype=jnp.float32)
    frequency = jnp.exp(-jnp.log(10000.0) * step_index / half_width)
    angles = positions.astype(jnp.float32)[:, None] * frequency[None, :]
    if values.ndim == 3:
        angles = angles[:, None, :]
    cosine = jnp.cos(angles)
    sine_part = jnp.sin(angles)
    first_half = values[..., :half_width]
    second = values[..., half_width:]
    return jnp.concatenate(
        [first_half * cosine - second * sine_part, second * cosine + first_half * sine_part],
        axis=-1,
    )


def slot_targets(expert_ids, block_rows):
    row_count, top_count = expert_ids.shape
    blocks = row_count // block_rows
    flat_ids = expert_ids.reshape(blocks, block_rows * top_count)
    onehot = (flat_ids[:, :, None] == jnp.arange(EXPERTS, dtype=jnp.int32)[None, None, :]).astype(
        jnp.int32
    )
    earlier = jnp.cumsum(onehot, axis=1) - onehot
    rank_in = jnp.sum(earlier * onehot, axis=2)
    capacity = blocks * MOST
    target = flat_ids * capacity + jnp.arange(blocks, dtype=jnp.int32)[:, None] * MOST + rank_in
    return (target.reshape(row_count, top_count), capacity)


def pack_rows(source, target, capacity):
    slot_count = EXPERTS * capacity
    hit_table = (
        target[:, :, None] == jnp.arange(slot_count, dtype=jnp.int32)[None, None, :]
    ).astype(jnp.bfloat16)
    hit_table = jnp.sum(hit_table, axis=1)
    packed = lax.dot_general(
        hit_table, source, (((0,), (0,)), ((), ())), preferred_element_type=jnp.float32
    )
    return packed.astype(jnp.bfloat16)


def expert_part(slot_rows, w_gate_up, w_down):
    gate_up = jnp.einsum(
        "secx,egfx->secgf", slot_rows, w_gate_up, preferred_element_type=jnp.float32
    )
    activated = (jax.nn.silu(gate_up[:, :, :, 0, :]) * gate_up[:, :, :, 1, :]).astype(jnp.bfloat16)
    return jnp.einsum("secf,efx->secx", activated, w_down, preferred_element_type=jnp.float32)


def combine_rows(middle, expert_out, target, route_weights):
    flat_out = expert_out.reshape(-1, expert_out.shape[-1])
    routed = jnp.take(flat_out, target.reshape(-1), axis=0)
    routed = routed.reshape(target.shape + (flat_out.shape[1],)).astype(jnp.float32)
    layer_out = middle.astype(jnp.float32) + jnp.sum(route_weights[:, :, None] * routed, axis=1)
    return layer_out.astype(jnp.bfloat16)


def attend(
    query_latent, query_rope, latent_new, key_new, latent_cache, rope_cache, lengths, score_scale
):
    scores = jnp.einsum(
        "rhl,rtl->rht", query_latent, latent_cache, preferred_element_type=jnp.float32
    )
    scores = scores + jnp.einsum(
        "rhp,rpt->rht", query_rope, rope_cache, preferred_element_type=jnp.float32
    )
    scores = scores * score_scale
    self_score = jnp.einsum(
        "rhl,rl->rh", query_latent, latent_new, preferred_element_type=jnp.float32
    )
    self_score = (
        self_score
        + jnp.einsum("rhp,rp->rh", query_rope, key_new, preferred_element_type=jnp.float32)
    ) * score_scale
    places = jnp.arange(latent_cache.shape[1], dtype=jnp.int32)
    valid_mask = places[None, None, :] < lengths[:, None, None]
    masked = jnp.where(valid_mask, scores, far_below)
    peak_score = jnp.maximum(jnp.max(masked, axis=2), self_score)
    weights = jnp.where(valid_mask, jnp.exp(masked - peak_score[:, :, None]), 0.0)
    self_weight = jnp.exp(self_score - peak_score)
    totals = jnp.sum(weights, axis=2) + self_weight
    prob_cache = (weights / totals[:, :, None]).astype(jnp.bfloat16)
    prob_self = (self_weight / totals).astype(jnp.bfloat16)
    mixed = jnp.einsum("rht,rtl->rhl", prob_cache, latent_cache, preferred_element_type=jnp.float32)
    mixed = (
        mixed
        + prob_self.astype(jnp.float32)[:, :, None] * latent_new.astype(jnp.float32)[:, None, :]
    )
    return mixed.astype(jnp.bfloat16)


def per_device(
    hidden,
    lengths,
    attn_gain,
    w_query,
    w_latent,
    latent_gain,
    w_rope_key,
    w_key_up,
    w_value_up,
    w_out,
    latent_cache,
    rope_cache,
    ffn_gain,
    expert_ids,
    route_weights,
    w_gate_up,
    w_down,
):
    sections = lax.axis_size("section")
    devices = lax.axis_size("dev")
    row_count = hidden.shape[0]
    quarter = row_count // sections
    model_width = hidden.shape[1]
    head_local = w_key_up.shape[0]
    nope_width = w_key_up.shape[2]
    rope_width = w_rope_key.shape[0]
    score_scale = (nope_width + rope_width) ** (-0.5)
    normed = rms_norm(hidden.astype(jnp.float32), attn_gain).astype(jnp.bfloat16)
    queries = jnp.dot(normed, w_query, preferred_element_type=jnp.float32).astype(jnp.bfloat16)
    queries = queries.reshape(row_count, head_local, nope_width + rope_width)
    query_rope = rotary(queries[:, :, nope_width:].astype(jnp.float32), lengths).astype(
        jnp.bfloat16
    )
    query_latent = jnp.einsum(
        "rhn,hln->rhl", queries[:, :, :nope_width], w_key_up, preferred_element_type=jnp.float32
    ).astype(jnp.bfloat16)
    latent_new = rms_norm(
        jnp.dot(normed, w_latent, preferred_element_type=jnp.float32), latent_gain
    ).astype(jnp.bfloat16)
    key_raw = lax.dot_general(
        normed, w_rope_key, (((1,), (1,)), ((), ())), preferred_element_type=jnp.float32
    )
    key_new = rotary(key_raw, lengths).astype(jnp.bfloat16)
    mixed_latent = attend(
        query_latent,
        query_rope,
        latent_new,
        key_new,
        latent_cache,
        rope_cache,
        lengths,
        score_scale,
    )
    head_out = jnp.einsum(
        "rhl,hlv->rhv", mixed_latent, w_value_up, preferred_element_type=jnp.float32
    ).astype(jnp.bfloat16)
    heads_flat = head_out.reshape(row_count, -1)
    partial_value = jnp.dot(heads_flat, w_out, preferred_element_type=jnp.float32)
    attention = lax.psum(partial_value, "section")
    middle = (hidden.astype(jnp.float32) + attention).astype(jnp.bfloat16)
    expert_in = rms_norm(middle.astype(jnp.float32), ffn_gain).astype(jnp.bfloat16)
    target, capacity = slot_targets(expert_ids, quarter)
    packed = pack_rows(expert_in, target, capacity).reshape(devices, -1, capacity, model_width)
    partial_out = expert_part(
        lax.all_to_all(packed, "dev", split_axis=0, concat_axis=0, tiled=True), w_gate_up, w_down
    )
    returned = lax.all_to_all(
        partial_out.astype(jnp.bfloat16), "dev", split_axis=0, concat_axis=0, tiled=True
    ).astype(partial_out.dtype)
    expert_out = lax.psum(returned.astype(jnp.bfloat16), "section")
    return combine_rows(middle, expert_out, target, route_weights)


def solution(mesh):
    in_specs = (
        P("dev", None),
        P("dev"),
        P(),
        P(None, "section"),
        P(),
        P(),
        P(),
        P("section", None, None),
        P("section", None, None),
        P("section", None),
        P("dev", None, None),
        P("dev", None, None),
        P(),
        P("dev", None),
        P("dev", None),
        P("dev", None, "section", None),
        P("dev", "section", None),
    )
    out_specs = P("dev", None)
    return jax.shard_map(
        per_device, mesh=mesh, in_specs=in_specs, out_specs=out_specs, check_vma=False
    )
```

profile of v0, /device:TPU:1, one launch (start us, length us, event | category | flops | bytes accessed | tf_op | source)
XLA Modules:
  0.0 220.6 jit_solution(4492424188257684018)
XLA Ops:
  6.6 0.5 multiply_exponential_fusion
  7.1 1.3 fusion.22
  8.5 2.2 %convolution_convert_fusion.3 = bf16[32,768]{1,0:T(8,128)(2,1)} fusion(bf16[2048,768]{1,0:T(8,128)(2,1)S(1)} %copy-done, bf16[32,2048]{1,0:T(8,128)(2,1)} %param.17, f32[2048]{0:T(1024)} %param.19, f32[32]{0:T(128)S(1)} %add_rsqrt_fusion.2), kind=kOutput, calls=%fused_computation.17 | convolution fusion | flops 100950016 | bytes 3334272 | tf_op jit(solution)/shard_map/dot_general | solution.py:139
  10.7 1.5 reshape.195
  12.3 0.9 slice_convert_fusion
  13.3 0.3 fusion.59
  13.6 0.9 subtract_convert_fusion.1
  14.7 0.2 fusion.49
  14.9 1.5 fusion.56
  16.5 0.6 multiply_reduce_fusion.1
  17.1 0.3 fusion.13
  17.5 0.2 fusion.35
  17.8 5.9 %fusion.65 = (f32[32,4]{1,0:T(8,128)S(1)}, f32[32,4,256]{2,1,0:T(4,128)S(1)}) fusion(f32[32,4,256]{2,1,0:T(4,128)S(1)} %fusion.56, bf16[32,256,512]{2,1,0:T(8,128)(2,1)} %param.27, bf16[32,4,512]{2,0,1:T(8,128)(2,1)S(1)} %fusion.13, pred[32,256]{1,0:T(8,128)(4,1)S(1)} %iota_compare_fusion.2), kind=kOutput, calls=%fused_computation.101 | convolution fusion | flops 33685376 | bytes 8790528 | tf_op jit(solution)/shard_map/rhl,rtl->rht/dot_general | solution.py:79
  23.7 0.2 fusion.39
  24.0 1.2 fusion.12
  25.4 0.3 copy-done.2
  25.7 1.2 fusion.45
  27.4 0.2 select_reduce_fusion
  28.1 41.6 %all-reduce.3.cloned.1.call-done = f32[32,2048]{1,0:T(8,128)} async-done(((f32[32,2048]{1,0:T(8,128)}), f32[32,2048]{1,0:T(8,128)}) %all-reduce.3.cloned.1.call-update) | async-done | bytes 262160 | tf_op jit(solution)/shard_map/psum | solution.py:169
  69.7 1.1 fusion.26
  70.9 0.8 convolution_convert_fusion
  71.6 37.8 %all_to_all.10 = bf16[32,2,8,2048]{3,2,1,0:T(8,128)(2,1)S(1)} all-to-all(bf16[32,2,8,2048]{3,2,1,0:T(8,128)(2,1)S(1)} %bitcast.68), channel_id=1, replica_groups=mesh['section'=4,'dev'=32] {'dev'}, dimensions={0} | all-to-all | bytes 4194304 | tf_op jit(solution)/shard_map/all_to_all | solution.py:175
  109.4 4.8 %fusion.7 = f32[32,2,8,2,352]{4,2,3,0,1:T(8,128)S(1)} fusion(bf16[2,2,352,2048]{3,2,1,0:T(8,128)(2,1)} %param.32, bf16[32,2,8,2048]{3,2,1,0:T(8,128)(2,1)S(1)} %all_to_all.10), kind=kOutput, calls=%fused_computation.9 | convolution fusion | flops 1476395008 | bytes 9306112 | tf_op jit(solution)/shard_map/secx,egfx->secgf/dot_general | solution.py:61
  114.2 1.3 fusion.3
  115.5 0.2 copy.56
  115.8 32.0 %all_to_all.11 = bf16[32,2,8,2048]{3,2,1,0:T(8,128)(2,1)} all-to-all(bf16[32,2,8,2048]{3,2,1,0:T(8,128)(2,1)S(1)} %copy.56), channel_id=1, replica_groups=mesh['section'=4,'dev'=32] {'dev'}, dimensions={0} | all-to-all | bytes 4194304 | tf_op jit(solution)/shard_map/all_to_all | solution.py:177
  148.1 0.3 copy-done.10
  148.6 54.8 %all-reduce.5.cloned.1.call-done = bf16[512,2048]{1,0:T(8,128)(2,1)} async-done(((bf16[512,2048]{1,0:T(8,128)(2,1)}), bf16[512,2048]{1,0:T(8,128)(2,1)}) %all-reduce.5.cloned.1.call-update) | async-done | bytes 2097168 | tf_op jit(solution)/shard_map/psum | solution.py:180
  203.3 4.7 %gather_fusion = bf16[192,2048]{1,0:T(8,128)(2,1)} fusion(bf16[512,2048]{1,0:T(8,128)(2,1)} %all-reduce.5.cloned.1.call-done, s32[1024]{0:T(1024)S(1)} %pad_clamp_fusion), kind=kCustom, calls=%fused_computation | custom fusion | bytes 1573632 | tf_op jit(solution)/shard_map/jit(_take)/gather | solution.py:70
  208.0 2.2 gather.7
  210.2 2.9 %multiply_reduce_fusion = f32[32,2048]{1,0:T(8,128)S(1)} fusion(bf16[32,6,2048]{2,1,0:T(8,128)(2,1)} %gather.7, f32[32,6]{1,0:T(8,128)S(1)} %copy.50, pred[32,6]{1,0:T(8,128)(4,1)S(1)} %get-tuple-element.5), kind=kLoop, calls=%fused_computation.8 | loop fusion | flops 1507328 | bytes 1049536 | tf_op jit(solution)/shard_map/reduce_sum | solution.py:72
  213.1 0.7 fusion.29
  (67 shorter events, 2.2 us)
Async XLA Ops:
  6.5 2.0 copy-start
  6.5 6.8 %copy-start.1 = (bf16[32,2048]{1,0:T(8,128)(2,1)S(1)}, bf16[32,2048]{1,0:T(8,128)(2,1)}, u32[]{:S(2)}) copy-start(bf16[32,2048]{1,0:T(8,128)(2,1)} %param.17) | copy-start | bytes 393220
  6.5 6.8 %copy-start.7 = (f32[2048]{0:T(1024)S(1)}, f32[2048]{0:T(1024)}, u32[]{:S(2)}) copy-start(f32[2048]{0:T(1024)} %param.19) | copy-start | bytes 24580
  6.5 6.6 %copy-start.12 = (s32[32]{0:T(128)S(1)}, s32[32]{0:T(128)}, u32[]{:S(2)}) copy-start(s32[32]{0:T(128)} %param.18) | copy-start | bytes 388
  6.5 6.8 %copy-start.6 = (bf16[64,2048]{1,0:T(8,128)(2,1)S(1)}, bf16[64,2048]{1,0:T(8,128)(2,1)}, u32[]{:S(2)}) copy-start(bf16[64,2048]{1,0:T(8,128)(2,1)} %param.23) | copy-start | bytes 786436
  6.5 63.2 %all-reduce.3.cloned.1.call-start = ((), (), s32[]{:S(2)}) async-start(), calls=%async_computation.2 | async-start | bytes 524288 | tf_op jit(solution)/shard_map/psum | solution.py:169
  12.3 4.2 %copy-start.3 = (bf16[2048,512]{1,0:T(8,128)(2,1)S(1)}, bf16[2048,512]{1,0:T(8,128)(2,1)}, u32[]{:S(2)}) copy-start(bf16[2048,512]{1,0:T(8,128)(2,1)} %param.21) | copy-start | bytes 6291460
  12.3 5.2 %copy-start.11 = (f32[512]{0:T(512)S(1)}, f32[512]{0:T(512)}, u32[]{:S(2)}) copy-start(f32[512]{0:T(512)} %param.22) | copy-start | bytes 6148
  13.2 3.9 %copy-start.4 = (bf16[4,512,128]{2,1,0:T(8,128)(2,1)S(1)}, bf16[4,512,128]{2,1,0:T(8,128)(2,1)}, u32[]{:S(2)}) copy-start(bf16[4,512,128]{2,1,0:T(8,128)(2,1)} %param.24) | copy-start | bytes 1572868
  13.2 3.9 %slice-start.2 = ((bf16[32,4,192]{2,1,0:T(4,128)(2,1)}), bf16[32,4,128]{2,1,0:T(4,128)(2,1)S(1)}, s32[]{:S(2)}) async-start(bf16[32,4,192]{2,1,0:T(4,128)(2,1)} %reshape.195), calls=%async_computation.6 | async-start | bytes 65536 | tf_op jit(solution)/shard_map/slice | solution.py:145
  13.3 10.6 %slice-start = ((s8[8388608]{0:T(1024)(128)(4,1)}), s8[4194304]{0:T(1024)(128)(4,1)S(1)}, s32[]{:S(2)}) async-start(s8[8388608]{0:T(1024)(128)(4,1)} %bitcast.65), calls=%async_computation.4 | async-start | bytes 8388608
  17.8 6.2 %slice-start.1 = ((s8[8388608]{0:T(1024)(128)(4,1)}), s8[4194304]{0:T(1024)(128)(4,1)S(1)}, s32[]{:S(2)}) async-start(s8[8388608]{0:T(1024)(128)(4,1)} %bitcast.65), calls=%async_computation.5 | async-start | bytes 8388608
  23.9 1.3 copy-start.5
  24.0 1.8 copy-start.2
  25.2 1.8 copy-start.9
  25.2 45.6 %copy-start.8 = (f32[2048]{0:T(1024)S(1)}, f32[2048]{0:T(1024)}, u32[]{:S(2)}) copy-start(f32[2048]{0:T(1024)} %param.29) | copy-start | bytes 24580
  26.9 176.4 %all-reduce.5.cloned.1.call-start = ((), (), s32[]{:S(2)}) async-start(), calls=%async_computation.3 | async-start | bytes 4194304 | tf_op jit(solution)/shard_map/psum | solution.py:180
  109.4 4.8 %copy-start.13 = (bf16[2,352,2048]{2,1,0:T(8,128)(2,1)S(1)}, bf16[2,352,2048]{2,1,0:T(8,128)(2,1)}, u32[]{:S(2)}) copy-start(bf16[2,352,2048]{2,1,0:T(8,128)(2,1)} %param.33) | copy-start | bytes 8650756
  147.8 0.7 copy-start.10
Sparse Core Ops, SparseCore 0:
  27.0 42.6 all-reduce.2
  147.9 55.3 all-reduce.4
where the time goes:
time: 221 us
  waiting for transfers between devices  96.4 us (44%)
  blocking collectives  69.8 us (32%)
  matrix products  20.7 us (9%)
  between operations  13.7 us (6%)
  local copies, waits for them, and re-layouts  10.3 us (5%)
  other arithmetic  9.69 us (4%)
    psum x1, waiting for transfers between devices, per_device(): expert_out = lax.psum(returned.astype(jnp.bfloat16), 'section')  54.8 us
    psum x1, waiting for transfers between devices, per_device(): attention = lax.psum(partial_value, 'section')  41.6 us
    all_to_all x1, blocking collectives, per_device(): lax.all_to_all(packed, 'dev', split_axis=0, concat_axis=0, tiled=True)  37.8 us
    all_to_all x1, blocking collectives, per_device(): lax.all_to_all(partial_out.astype(jnp.bfloat16), 'dev', split_axis=0, con...  32 us
    gather x2, local copies, waits for them, and re-layouts, combine_rows(): routed = jnp.take(flat_out, target.reshape(-1), axis=0)  6.85 us
    dot_general x1, matrix products, attend(): jnp.einsum('rhl,rtl->rht', query_latent, latent_cache, preferred_element_...  5.89 us
    dot_general x1, matrix products, expert_part(): jnp.einsum('secx,egfx->secgf', slot_rows, w_gate_up, preferred_element_ty...  4.8 us
  transfers between devices with their start and end apart: 2, of which 2 were waited for; matrix products, arithmetic and copies ran while one was open for 1% of the time, Pallas kernels for 0%

commit v1 on v0

--- a/solution.py
+++ b/solution.py
@@ -166,7 +166,7 @@
     ).astype(jnp.bfloat16)
     heads_flat = head_out.reshape(row_count, -1)
     partial_value = jnp.dot(heads_flat, w_out, preferred_element_type=jnp.float32)
-    attention = lax.psum(partial_value, "section")
+    attention = jnp.sum(lax.all_gather(partial_value, "section"), axis=0)
     middle = (hidden.astype(jnp.float32) + attention).astype(jnp.bfloat16)
     expert_in = rms_norm(middle.astype(jnp.float32), ffn_gain).astype(jnp.bfloat16)
     target, capacity = slot_targets(expert_ids, quarter)

time: 221 us -> 205 us (0.928)
  waiting for transfers between devices: 96.4 us -> 79.9 us
    psum x1 -> x0, waiting for transfers between devices: 41.6 us -> none  [per_device(): attention = lax.psum(partial_value, 'section')]
    all_gather x0 -> x1, waiting for transfers between devices: none -> 25.2 us  [per_device(): attention = jnp.sum(lax.all_gather(partial_value, 'section'), axis=0)]
where the time goes in v1:
time: 205 us
  waiting for transfers between devices  79.9 us (39%)
  blocking collectives  68.6 us (33%)
  matrix products  20.7 us (10%)
  between operations  13.7 us (7%)
  other arithmetic  11.7 us (6%)
  local copies, waits for them, and re-layouts  10.3 us (5%)
    psum x1, waiting for transfers between devices, per_device(): expert_out = lax.psum(returned.astype(jnp.bfloat16), 'section')  54.6 us
    all_to_all x1, blocking collectives, per_device(): lax.all_to_all(packed, 'dev', split_axis=0, concat_axis=0, tiled=True)  36.6 us
    all_to_all x1, blocking collectives, per_device(): lax.all_to_all(partial_out.astype(jnp.bfloat16), 'dev', split_axis=0, con...  32 us
    all_gather x1, waiting for transfers between devices, per_device(): attention = jnp.sum(lax.all_gather(partial_value, 'section'), axis=0)  25.2 us
    gather x2, local copies, waits for them, and re-layouts, combine_rows(): routed = jnp.take(flat_out, target.reshape(-1), axis=0)  6.85 us
    dot_general x1, matrix products, attend(): jnp.einsum('rhl,rtl->rht', query_latent, latent_cache, preferred_element_...  5.89 us
    dot_general x1, matrix products, expert_part(): jnp.einsum('secx,egfx->secgf', slot_rows, w_gate_up, preferred_element_ty...  4.8 us
  transfers between devices with their start and end apart: 2, of which 2 were waited for; matrix products, arithmetic and copies ran while one was open for 1% of the time, Pallas kernels for 0%

profile of v1, /device:TPU:1, one launch (start us, length us, event | category | flops | bytes accessed | tf_op | source)
XLA Modules:
  0.0 204.9 jit_solution(13336655803756708709)
XLA Ops:
  6.6 0.5 multiply_exponential_fusion
  7.1 1.3 fusion.22
  8.5 2.2 %convolution_convert_fusion.3 = bf16[32,768]{1,0:T(8,128)(2,1)} fusion(bf16[2048,768]{1,0:T(8,128)(2,1)S(1)} %copy-done, bf16[32,2048]{1,0:T(8,128)(2,1)} %param.17, f32[2048]{0:T(1024)} %param.19, f32[32]{0:T(128)S(1)} %add_rsqrt_fusion.2), kind=kOutput, calls=%fused_computation.17 | convolution fusion | flops 100950016 | bytes 3334272 | tf_op jit(solution)/shard_map/dot_general | solution.py:139
  10.7 1.5 reshape.195
  12.3 0.9 slice_convert_fusion
  13.3 0.3 fusion.59
  13.6 0.9 subtract_convert_fusion.1
  14.7 0.2 fusion.49
  14.9 1.5 fusion.56
  16.5 0.6 multiply_reduce_fusion.1
  17.1 0.3 fusion.13
  17.5 0.2 fusion.35
  17.8 5.9 %fusion.65 = (f32[32,4]{1,0:T(8,128)S(1)}, f32[32,4,256]{2,1,0:T(4,128)S(1)}) fusion(f32[32,4,256]{2,1,0:T(4,128)S(1)} %fusion.56, bf16[32,256,512]{2,1,0:T(8,128)(2,1)} %param.27, bf16[32,4,512]{2,0,1:T(8,128)(2,1)S(1)} %fusion.13, pred[32,256]{1,0:T(8,128)(4,1)S(1)} %iota_compare_fusion.2), kind=kOutput, calls=%fused_computation.101 | convolution fusion | flops 33685376 | bytes 8790528 | tf_op jit(solution)/shard_map/rhl,rtl->rht/dot_general | solution.py:79
  24.0 1.2 fusion.12
  25.4 0.3 copy-done.2
  25.7 1.2 fusion.45
  27.4 0.2 select_reduce_fusion
  28.1 25.2 %all-gather.3.cloned.1.call-done = f32[128,2048]{1,0:T(8,128)} async-done(((f32[32,2048]{1,0:T(8,128)}), f32[128,2048]{1,0:T(8,128)}) %all-gather.3.cloned.1.call-update) | async-done | bytes 1048592 | tf_op jit(solution)/shard_map/all_gather | solution.py:169
  53.4 2.0 reduce_sum.82
  55.4 1.1 fusion.26
  56.5 0.8 convolution_convert_fusion
  57.3 36.6 %all_to_all.10 = bf16[32,2,8,2048]{3,2,1,0:T(8,128)(2,1)S(1)} all-to-all(bf16[32,2,8,2048]{3,2,1,0:T(8,128)(2,1)S(1)} %bitcast.69), channel_id=1, replica_groups=mesh['section'=4,'dev'=32] {'dev'}, dimensions={0} | all-to-all | bytes 4194304 | tf_op jit(solution)/shard_map/all_to_all | solution.py:175
  93.8 4.8 %fusion.7 = f32[32,2,8,2,352]{4,2,3,0,1:T(8,128)S(1)} fusion(bf16[2,2,352,2048]{3,2,1,0:T(8,128)(2,1)} %param.32, bf16[32,2,8,2048]{3,2,1,0:T(8,128)(2,1)S(1)} %all_to_all.10), kind=kOutput, calls=%fused_computation.9 | convolution fusion | flops 1476395008 | bytes 9306112 | tf_op jit(solution)/shard_map/secx,egfx->secgf/dot_general | solution.py:61
  98.7 1.3 fusion.3
  100.0 0.2 copy.56
  100.2 32.0 %all_to_all.11 = bf16[32,2,8,2048]{3,2,1,0:T(8,128)(2,1)} all-to-all(bf16[32,2,8,2048]{3,2,1,0:T(8,128)(2,1)S(1)} %copy.56), channel_id=1, replica_groups=mesh['section'=4,'dev'=32] {'dev'}, dimensions={0} | all-to-all | bytes 4194304 | tf_op jit(solution)/shard_map/all_to_all | solution.py:177
  132.6 0.3 copy-done.10
  133.0 54.6 %all-reduce.2.cloned.1.call-done = bf16[512,2048]{1,0:T(8,128)(2,1)} async-done(((bf16[512,2048]{1,0:T(8,128)(2,1)}), bf16[512,2048]{1,0:T(8,128)(2,1)}) %all-reduce.2.cloned.1.call-update) | async-done | bytes 2097168 | tf_op jit(solution)/shard_map/psum | solution.py:180
  187.6 4.7 %gather_fusion = bf16[192,2048]{1,0:T(8,128)(2,1)} fusion(bf16[512,2048]{1,0:T(8,128)(2,1)} %all-reduce.2.cloned.1.call-done, s32[1024]{0:T(1024)S(1)} %pad_clamp_fusion), kind=kCustom, calls=%fused_computation | custom fusion | bytes 1573632 | tf_op jit(solution)/shard_map/jit(_take)/gather | solution.py:70
  192.3 2.2 %gather.7 = bf16[32,6,2048]{2,1,0:T(8,128)(2,1)} reshape(bf16[192,2048]{1,0:T(8,128)(2,1)} %gather_fusion) | data formatting | bytes 1572864 | tf_op jit(solution)/shard_map/jit(_take)/gather | solution.py:70
  194.5 2.9 %multiply_reduce_fusion = f32[32,2048]{1,0:T(8,128)S(1)} fusion(bf16[32,6,2048]{2,1,0:T(8,128)(2,1)} %gather.7, f32[32,6]{1,0:T(8,128)S(1)} %copy.50, pred[32,6]{1,0:T(8,128)(4,1)S(1)} %get-tuple-element.5), kind=kLoop, calls=%fused_computation.8 | loop fusion | flops 1507328 | bytes 1049536 | tf_op jit(solution)/shard_map/reduce_sum | solution.py:72
  197.4 0.7 fusion.29
  (68 shorter events, 2.4 us)
Async XLA Ops:
  6.5 2.0 copy-start
  6.5 6.8 %copy-start.1 = (bf16[32,2048]{1,0:T(8,128)(2,1)S(1)}, bf16[32,2048]{1,0:T(8,128)(2,1)}, u32[]{:S(2)}) copy-start(bf16[32,2048]{1,0:T(8,128)(2,1)} %param.17) | copy-start | bytes 393220
  6.5 6.8 %copy-start.7 = (f32[2048]{0:T(1024)S(1)}, f32[2048]{0:T(1024)}, u32[]{:S(2)}) copy-start(f32[2048]{0:T(1024)} %param.19) | copy-start | bytes 24580
  6.5 6.6 %copy-start.12 = (s32[32]{0:T(128)S(1)}, s32[32]{0:T(128)}, u32[]{:S(2)}) copy-start(s32[32]{0:T(128)} %param.18) | copy-start | bytes 388
  6.5 6.8 %copy-start.6 = (bf16[64,2048]{1,0:T(8,128)(2,1)S(1)}, bf16[64,2048]{1,0:T(8,128)(2,1)}, u32[]{:S(2)}) copy-start(bf16[64,2048]{1,0:T(8,128)(2,1)} %param.23) | copy-start | bytes 786436
  6.5 46.8 %all-gather.3.cloned.1.call-start = ((), (), s32[]{:S(2)}) async-start(), calls=%async_computation.3 | async-start | bytes 1310720 | tf_op jit(solution)/shard_map/all_gather | solution.py:169
  12.3 4.2 %copy-start.3 = (bf16[2048,512]{1,0:T(8,128)(2,1)S(1)}, bf16[2048,512]{1,0:T(8,128)(2,1)}, u32[]{:S(2)}) copy-start(bf16[2048,512]{1,0:T(8,128)(2,1)} %param.21) | copy-start | bytes 6291460
  12.3 5.2 %copy-start.11 = (f32[512]{0:T(512)S(1)}, f32[512]{0:T(512)}, u32[]{:S(2)}) copy-start(f32[512]{0:T(512)} %param.22) | copy-start | bytes 6148
  13.2 3.9 %copy-start.4 = (bf16[4,512,128]{2,1,0:T(8,128)(2,1)S(1)}, bf16[4,512,128]{2,1,0:T(8,128)(2,1)}, u32[]{:S(2)}) copy-start(bf16[4,512,128]{2,1,0:T(8,128)(2,1)} %param.24) | copy-start | bytes 1572868
  13.2 3.9 %slice-start.2 = ((bf16[32,4,192]{2,1,0:T(4,128)(2,1)}), bf16[32,4,128]{2,1,0:T(4,128)(2,1)S(1)}, s32[]{:S(2)}) async-start(bf16[32,4,192]{2,1,0:T(4,128)(2,1)} %reshape.195), calls=%async_computation.6 | async-start | bytes 65536 | tf_op jit(solution)/shard_map/slice | solution.py:145
  13.3 10.6 %slice-start = ((s8[8388608]{0:T(1024)(128)(4,1)}), s8[4194304]{0:T(1024)(128)(4,1)S(1)}, s32[]{:S(2)}) async-start(s8[8388608]{0:T(1024)(128)(4,1)} %bitcast.66), calls=%async_computation.4 | async-start | bytes 8388608
  17.8 6.2 %slice-start.1 = ((s8[8388608]{0:T(1024)(128)(4,1)}), s8[4194304]{0:T(1024)(128)(4,1)S(1)}, s32[]{:S(2)}) async-start(s8[8388608]{0:T(1024)(128)(4,1)} %bitcast.66), calls=%async_computation.5 | async-start | bytes 8388608
  23.9 1.3 copy-start.5
  24.0 1.8 copy-start.2
  25.2 1.8 copy-start.9
  25.7 30.8 %copy-start.8 = (f32[2048]{0:T(1024)S(1)}, f32[2048]{0:T(1024)}, u32[]{:S(2)}) copy-start(f32[2048]{0:T(1024)} %param.29) | copy-start | bytes 24580
  26.9 160.7 %all-reduce.2.cloned.1.call-start = ((), (), s32[]{:S(2)}) async-start(), calls=%async_computation.2 | async-start | bytes 4194304 | tf_op jit(solution)/shard_map/psum | solution.py:180
  93.8 4.8 %copy-start.13 = (bf16[2,352,2048]{2,1,0:T(8,128)(2,1)S(1)}, bf16[2,352,2048]{2,1,0:T(8,128)(2,1)}, u32[]{:S(2)}) copy-start(bf16[2,352,2048]{2,1,0:T(8,128)(2,1)} %param.33) | copy-start | bytes 8650756
  132.2 0.7 copy-start.10
Sparse Core Ops, SparseCore 0:
  27.1 26.2 all-gather.2
  132.3 55.2 all-reduce.1
